TPU v7x, 256 devices: a whole 4x4x8 slice. The times are simulated.
256 devices in a mesh: dp: 4 (over x), space: 16 (over z_lo, y), tm: 4 (over z_hi, core).
Axes of the slice: x: 4, y: 4, z: 8 (z_hi: 2, z_lo: 4; z = z_hi * 4 + z_lo), core: 2. Of those that a mesh axis runs over, the one named last changes fastest.
Arguments:
- inputs: bfloat16 [4, 32, 64, 4096], P('dp', 'tm', None, 'space'), may hold values from -6 to 6
- grad_out: bfloat16 [4, 32, 64, 4096], P('dp', 'tm', None, 'space'), may hold values from -6 to 6
- conv_w: bfloat16 [2, 128, 64], replicated, may hold values from -0.5 to 0.5
- conv_b: float32 [128], replicated, may hold values from -3 to 3
- mix_w: bfloat16 [3, 64, 64], replicated, may hold values from -0.4375 to 0.4375
- mix_b: float32 [64], replicated, may hold values from -3 to 3
- adj_tiles: bfloat16 [32, 8, 128, 128], P('space'), may hold values from -0.1875 to 0.1875
- tile_cols: int32 [32, 8], P('space'), may hold values from 0 to 9, as said below
- send_rows: int32 [16, 16, 64], P('space'), may hold values from 0 to 255
- counts: int32 [16, 16], P('space'), may hold values from 0 to 64, as said below
Outputs:
- outputs: bfloat16 [4, 32, 64, 4096], P('dp', 'tm', None, 'space')
- grad_inputs: bfloat16 [4, 32, 64, 4096], P('dp', 'tm', None, 'space')
- grad_conv_w: float32 [2, 128, 64], replicated
- grad_conv_b: float32 [128], replicated
- grad_mix_w: float32 [3, 64, 64], replicated
- grad_mix_b: float32 [64], replicated
Inputs may be any that keep to these rules, and one draw needn't show every extreme that they name: counts[s, s] = 0; counts[0, 1] = 64. `tile_cols`: column blocks below 2 are the part's own sensor blocks, 2 + i the i-th block of 128 received slots in order of source part and slot; in each row block the first 4 ids are below 2, the others are not.
All inputs are finite; a program needn't handle non-finite values.
Results may differ from a plain program's by a relative error of at most 0.0058.
Values may be sent and summed in bfloat16 or wider, within the bound.
A program may use at most 64 MiB of HBM per device.

v0:
```python
import math
import jax
import jax.numpy as jnp
from jax import lax
from jax.sharding import PartitionSpec as P

DILATION_SIZE = 2


def from_behind(value, axis, steps):
    count = lax.axis_size(axis)
    leading, last = (max(0, -steps), min(count, count - steps))
    return lax.ppermute(value, axis, [(source, source + steps) for source in range(leading, last)])


def slot_mask(counts, slot_count, dtype):
    slots = lax.broadcasted_iota(jnp.int32, (counts.shape[1], slot_count), 1)
    return (slots < counts[0][:, None]).astype(dtype)


def pack_rows(field, send_rows, live_slots):
    picked = field[:, :, send_rows[0]] * live_slots
    return picked.reshape(field.shape[0], field.shape[1], -1)


def tile_product(extended, adj_tiles, tile_cols):
    timestep_count, chan_count = (extended.shape[0], extended.shape[1])
    blocks = extended.reshape(timestep_count, chan_count, -1, adj_tiles.shape[2])
    picked = blocks[:, :, tile_cols]
    return jnp.einsum("tcrkj,rkij->tcri", picked, adj_tiles, preferred_element_type=jnp.float32)


def forward_start(field, send_rows, live_slots):
    packed = pack_rows(field, send_rows, live_slots)
    own_part = None
    return (packed, own_part)


def forward_finish(field, received, adj_tiles, tile_cols):
    total = tile_product(jnp.concatenate([field, received], 2), adj_tiles, tile_cols)
    return total.reshape(field.shape).astype(jnp.bfloat16)


def back_start(grad, adj_tiles, tile_cols, send_rows):
    timestep_count, chan_count, sensor_count = grad.shape
    tile_size = adj_tiles.shape[2]
    row_blocks = sensor_count // tile_size
    half_slots = tile_cols.shape[1] // 2
    halo_blocks = send_rows.shape[1] * send_rows.shape[2] // tile_size
    blocks = grad.reshape(timestep_count, chan_count, row_blocks, tile_size)
    remote_terms = jnp.einsum(
        "tcri,rkij->tcrkj", blocks, adj_tiles[:, half_slots:], preferred_element_type=jnp.float32
    )
    remote_sums = jnp.zeros((timestep_count, chan_count, halo_blocks, tile_size), jnp.float32)
    remote_sums = remote_sums.at[:, :, tile_cols[:, half_slots:] - row_blocks].add(remote_terms)
    return remote_sums.reshape(timestep_count, chan_count, -1).astype(jnp.bfloat16)


def back_finish(grad, returned, adj_tiles, tile_cols, send_rows, live_slots):
    timestep_count, chan_count, sensor_count = grad.shape
    tile_size = adj_tiles.shape[2]
    row_blocks = sensor_count // tile_size
    half_slots = tile_cols.shape[1] // 2
    blocks = grad.reshape(timestep_count, chan_count, row_blocks, tile_size)
    own_terms = jnp.einsum(
        "tcri,rkij->tcrkj", blocks, adj_tiles[:, :half_slots], preferred_element_type=jnp.float32
    )
    total = jnp.zeros((timestep_count, chan_count, row_blocks, tile_size), jnp.float32)
    total = total.at[:, :, tile_cols[:, :half_slots]].add(own_terms).reshape(grad.shape)
    returned = returned.reshape(
        timestep_count, chan_count, send_rows.shape[1], send_rows.shape[2]
    ).astype(jnp.float32)
    return total.at[:, :, send_rows[0]].add(returned * live_slots.astype(jnp.float32))


def mixing_grads(sample_grad, fields):
    grad_mix_w = jnp.stack(
        [
            jnp.einsum("ton,tcn->oc", sample_grad, item, preferred_element_type=jnp.float32)
            for item in fields
        ]
    )
    grad_mix_b = jnp.sum(sample_grad.astype(jnp.float32), axis=(0, 2))
    return (grad_mix_w, grad_mix_b)


def body(inputs, grad_out, conv_w, conv_b, mix_w, mix_b, adj_tiles, tile_cols, send_rows, counts):
    sample_input = inputs[0]
    sample_grad = grad_out[0]
    timestep_count, chan_count, sensor_count = sample_input.shape
    live_slots = slot_mask(counts, send_rows.shape[2], jnp.bfloat16)
    prior_border_slice = from_behind(sample_input[timestep_count - DILATION_SIZE :], "tm", 1)
    preceding_window = jnp.concatenate(
        [prior_border_slice, sample_input[: timestep_count - DILATION_SIZE]], 0
    )
    preact = jnp.einsum("oc,tcn->ton", conv_w[1], sample_input, preferred_element_type=jnp.float32)
    preact = preact + jnp.einsum(
        "oc,tcn->ton", conv_w[0], preceding_window, preferred_element_type=jnp.float32
    )
    preact = preact + conv_b[None, :, None]
    filtered = jnp.tanh(preact[:, :chan_count])
    gating = jax.nn.sigmoid(preact[:, chan_count:])
    hidden = (filtered * gating).astype(jnp.bfloat16)
    grad_float = sample_grad.astype(jnp.float32)
    packed_one, early_one = forward_start(hidden, send_rows, live_slots)
    received_one = lax.all_to_all(packed_one, "space", split_axis=2, concat_axis=2, tiled=True)
    hop_one = forward_finish(hidden, received_one, adj_tiles, tile_cols)
    packed_two, early_two = forward_start(hop_one, send_rows, live_slots)
    received_two = lax.all_to_all(packed_two, "space", split_axis=2, concat_axis=2, tiled=True)
    hop_two = forward_finish(hop_one, received_two, adj_tiles, tile_cols)
    fields = (hidden, hop_one, hop_two)
    grad_mix_w, grad_mix_b = mixing_grads(sample_grad, fields)
    back_two = jnp.einsum(
        "oc,ton->tcn", mix_w[2], sample_grad, preferred_element_type=jnp.float32
    ).astype(jnp.bfloat16)
    returned_two = lax.all_to_all(
        back_start(back_two, adj_tiles, tile_cols, send_rows),
        "space",
        split_axis=2,
        concat_axis=2,
        tiled=True,
    )
    back_one = jnp.einsum("oc,ton->tcn", mix_w[1], sample_grad, preferred_element_type=jnp.float32)
    back_one = (
        back_one + back_finish(back_two, returned_two, adj_tiles, tile_cols, send_rows, live_slots)
    ).astype(jnp.bfloat16)
    returned_one = lax.all_to_all(
        back_start(back_one, adj_tiles, tile_cols, send_rows),
        "space",
        split_axis=2,
        concat_axis=2,
        tiled=True,
    )
    back_hidden = jnp.einsum(
        "oc,ton->tcn", mix_w[0], sample_grad, preferred_element_type=jnp.float32
    )
    back_hidden = back_hidden + back_finish(
        back_one, returned_one, adj_tiles, tile_cols, send_rows, live_slots
    )
    mixed = sample_input.astype(jnp.float32) + mix_b[None, :, None]
    for index in range(3):
        mixed = mixed + jnp.einsum(
            "oc,tcn->ton", mix_w[index], fields[index], preferred_element_type=jnp.float32
        )
    outputs = mixed.astype(jnp.bfloat16)[None]
    grad_filter = back_hidden * (1.0 - filtered * filtered) * gating
    grad_gate = back_hidden * filtered * gating * (1.0 - gating)
    backward_preactivation = jnp.concatenate([grad_filter, grad_gate], 1).astype(jnp.bfloat16)
    next_border_slice = from_behind(backward_preactivation[:DILATION_SIZE], "tm", -1)
    following_window = jnp.concatenate(
        [backward_preactivation[DILATION_SIZE:], next_border_slice], 0
    )
    grad_inputs = grad_float + jnp.einsum(
        "oc,ton->tcn", conv_w[1], backward_preactivation, preferred_element_type=jnp.float32
    )
    grad_inputs = grad_inputs + jnp.einsum(
        "oc,ton->tcn", conv_w[0], following_window, preferred_element_type=jnp.float32
    )
    grad_inputs = grad_inputs.astype(jnp.bfloat16)[None]
    grad_conv_w = jnp.stack(
        [
            jnp.einsum(
                "ton,tcn->oc",
                backward_preactivation,
                preceding_window,
                preferred_element_type=jnp.float32,
            ),
            jnp.einsum(
                "ton,tcn->oc",
                backward_preactivation,
                sample_input,
                preferred_element_type=jnp.float32,
            ),
        ]
    )
    grad_conv_b = jnp.sum(backward_preactivation.astype(jnp.float32), axis=(0, 2))
    grad_conv_w, grad_conv_b, grad_mix_w, grad_mix_b = lax.psum(
        (grad_conv_w, grad_conv_b, grad_mix_w, grad_mix_b), ("dp", "space", "tm")
    )
    cell_count = (
        inputs.shape[0]
        * timestep_count
        * sensor_count
        * lax.axis_size("dp")
        * lax.axis_size("space")
        * lax.axis_size("tm")
    )
    scale = 1.0 / math.sqrt(cell_count)
    return (
        outputs,
        grad_inputs,
        grad_conv_w * scale,
        grad_conv_b * scale,
        grad_mix_w * scale,
        grad_mix_b * scale,
    )


def solution(mesh):
    in_specs = (
        P("dp", "tm", None, "space"),
        P("dp", "tm", None, "space"),
        P(),
        P(),
        P(),
        P(),
        P("space", None, None, None),
        P("space", None),
        P("space", None, None),
        P("space", None),
    )
    out_specs = (P("dp", "tm", None, "space"), P("dp", "tm", None, "space"), P(), P(), P(), P())
    return jax.shard_map(body, mesh=mesh, in_specs=in_specs, out_specs=out_specs, check_vma=False)
```

profile of v0, /device:TPU:1, one launch (start us, length us, event | category | flops | bytes accessed | tf_op | source)
XLA Modules:
  0.0 680.7 jit_solution(10881315894750508709)
XLA Ops:
  12.5 3.5 scatter_fusion.1
  19.6 9.2 %all-to-all-start.2 = ((bf16[16,2,16384]{2,1,0:T(2,128)(2,1)}), bf16[16,2,16384]{2,1,0:T(2,128)(2,1)}, u32[]{:S(2)}, u32[]{:S(2)}) async-start(bf16[16,2,16384]{2,1,0:T(2,128)(2,1)} %reshape.258), calls=%async_computation.2 | async-start | bytes 2097152 | tf_op jit(solution)/shard_map/all_to_all | solution.py:116
  32.5 18.7 %all-to-all-done.2 = bf16[16,2,16384]{2,1,0:T(2,128)(2,1)} async-done(((bf16[16,2,16384]{2,1,0:T(2,128)(2,1)}), bf16[16,2,16384]{2,1,0:T(2,128)(2,1)}, u32[]{:S(2)}, u32[]{:S(2)}) %all-to-all-start.2) | async-done | bytes 1048608 | tf_op jit(solution)/shard_map/all_to_all | solution.py:116
  51.2 3.8 reshape.259
  55.0 3.1 convert_multiply_fusion.1
  58.1 71.3 %scatter_fusion.2 = f32[8,64,256]{1,0,2:T(8,128)S(1)} fusion(f32[8,64,256]{1,0,2:T(8,128)S(1)} %copy.84, s32[1024]{0:T(1024)S(1)} %reshape.131, f32[1024,8,64]{2,1,0:T(8,128)} %bitcast.273), kind=kCustom, calls=%fused_computation.6 | custom fusion | flops 524288 | bytes 6295552 | tf_op jit(solution)/shard_map/scatter-add | solution.py:73
  132.5 3.5 scatter_fusion.4
  141.6 7.7 %all-to-all-start.3 = ((bf16[16,2,16384]{2,1,0:T(2,128)(2,1)}), bf16[16,2,16384]{2,1,0:T(2,128)(2,1)}, u32[]{:S(2)}, u32[]{:S(2)}) async-start(bf16[16,2,16384]{2,1,0:T(2,128)(2,1)} %reshape.260), calls=%async_computation.3 | async-start | bytes 2097152 | tf_op jit(solution)/shard_map/all_to_all | solution.py:127
  149.3 8.2 %collective-permute-start = (bf16[2,64,256]{2,1,0:T(8,128)(2,1)S(1)}, bf16[2,64,256]{2,1,0:T(8,128)(2,1)S(1)}, u32[]{:S(2)}, u32[]{:S(2)}) collective-permute-start(bf16[2,64,256]{2,1,0:T(8,128)(2,1)S(1)} %slice_bitcast_fusion.1), channel_id=1, source_target_pairs={{0,1},{1,2},{2,3},{4,5},{5,6},{6,7},{8,9},{9,10},{10,11},{12,13},{... | collective-permute-start | bytes 196616 | tf_op jit(solution)/shard_map/ppermute | solution.py:13
  158.2 7.7 %collective-permute-done = bf16[2,64,256]{2,1,0:T(8,128)(2,1)S(1)} collective-permute-done((bf16[2,64,256]{2,1,0:T(8,128)(2,1)S(1)}, bf16[2,64,256]{2,1,0:T(8,128)(2,1)S(1)}, u32[]{:S(2)}, u32[]{:S(2)}) %collective-permute-start) | collective-permute-done | bytes 65568 | tf_op jit(solution)/shard_map/ppermute | solution.py:13
  172.2 3.8 reshape.261
  175.9 3.1 convert_multiply_fusion
  179.0 71.3 %scatter_fusion.5 = f32[8,64,256]{1,0,2:T(8,128)S(1)} fusion(f32[8,64,256]{1,0,2:T(8,128)S(1)} %copy.92, s32[1024]{0:T(1024)S(1)} %reshape.131, f32[1024,8,64]{2,1,0:T(8,128)} %bitcast.272), kind=kCustom, calls=%fused_computation.9 | custom fusion | flops 524288 | bytes 6295552 | tf_op jit(solution)/shard_map/scatter-add | solution.py:73
  252.6 7.6 %gather_fusion = bf16[1024,8,64]{2,1,0:T(8,128)(2,1)} fusion(bf16[8,64,256]{1,0,2:T(8,128)(2,1)S(1)} %copy.63, s32[1024]{0:T(1024)S(1)} %broadcast_clamp_fusion), kind=kCustom, calls=%fused_computation | custom fusion | bytes 2101248 | tf_op jit(solution)/shard_map/gather | solution.py:22
  260.1 4.9 fusion.76
  267.3 7.9 %all-to-all-start = ((bf16[16,2,16384]{2,1,0:T(2,128)(2,1)}), bf16[16,2,16384]{2,1,0:T(2,128)(2,1)S(1)}, u32[]{:S(2)}, u32[]{:S(2)}) async-start(bf16[16,2,16384]{2,1,0:T(2,128)(2,1)} %reshape.254), calls=%async_computation | async-start | bytes 2097152 | tf_op jit(solution)/shard_map/all_to_all | solution.py:106
  276.1 21.2 %all-to-all-done = bf16[16,2,16384]{2,1,0:T(2,128)(2,1)S(1)} async-done(((bf16[16,2,16384]{2,1,0:T(2,128)(2,1)}), bf16[16,2,16384]{2,1,0:T(2,128)(2,1)S(1)}, u32[]{:S(2)}, u32[]{:S(2)}) %all-to-all-start) | async-done | bytes 1048608 | tf_op jit(solution)/shard_map/all_to_all | solution.py:106
  297.3 2.3 reshape.255
  299.7 3.4 pad_maximum_fusion
  303.1 3.4 copy.65
  306.5 2.3 gather_fusion.1
  309.9 3.3 gather_fusion.2
  313.2 4.8 fusion.77
  318.0 4.7 reshape.256
  322.7 7.9 %all-to-all-start.1 = ((bf16[16,2,16384]{2,1,0:T(2,128)(2,1)}), bf16[16,2,16384]{2,1,0:T(2,128)(2,1)S(1)}, u32[]{:S(2)}, u32[]{:S(2)}) async-start(bf16[16,2,16384]{2,1,0:T(2,128)(2,1)} %reshape.256), calls=%async_computation.1 | async-start | bytes 2097152 | tf_op jit(solution)/shard_map/all_to_all | solution.py:109
  336.4 4.1 collective-permute-start.1
  340.7 236.7 %all-reduce.3.cloned.1.call-done = f32[2,128,64]{1,2,0:T(8,128)} async-done(((f32[2,128,64]{1,2,0:T(8,128)}), f32[2,128,64]{1,2,0:T(8,128)}) %all-reduce.3.cloned.1.call-update) | async-done | bytes 65552 | tf_op jit(solution)/shard_map/psum | solution.py:177
  582.9 2.3 reshape.257
  585.3 3.4 pad_maximum_fusion.1
  588.7 3.4 copy.71
  592.1 2.3 gather_fusion.3
  597.1 75.0 %all-reduce = (f32[128]{0:T(128)S(1)}, f32[3,64,64]{1,2,0:T(8,128)S(1)}, f32[64]{0:T(128)S(1)}) all-reduce(f32[128]{0:T(128)S(1)} %convert_reduce_fusion, f32[3,64,64]{1,2,0:T(8,128)S(1)} %pad_maximum_fusion.6, f32[64]{0:T(128)S(1)} %convert_reduce_fusion.1), channel_id=1, replica_groups=mesh['dp'=4,'space'=16,'tm'=4] {'dp','space','tm'}, use_global_device_ids=true, to_apply=%region_8.0 | all-reduce | flops 12480 | bytes 99840 | tf_op jit(solution)/shard_map/psum | solution.py:177
  (135 shorter events, 50.1 us)
Async XLA Ops:
  17.3 11.6 %copy-start.1 = (bf16[2,8,128,128]{3,2,1,0:T(8,128)(2,1)S(1)}, bf16[2,8,128,128]{3,2,1,0:T(8,128)(2,1)}, u32[]{:S(2)}) copy-start(bf16[2,8,128,128]{3,2,1,0:T(8,128)(2,1)} %param.16) | copy-start | bytes 1572868
  19.6 31.6 %all-to-all-start.2 = ((bf16[16,2,16384]{2,1,0:T(2,128)(2,1)}), bf16[16,2,16384]{2,1,0:T(2,128)(2,1)}, u32[]{:S(2)}, u32[]{:S(2)}) async-start(bf16[16,2,16384]{2,1,0:T(2,128)(2,1)} %reshape.258), calls=%async_computation.2 | async-start | bytes 2097152 | tf_op jit(solution)/shard_map/all_to_all | solution.py:116
  29.7 1.9 copy-start
  29.7 1.9 copy-start.19
  31.6 0.8 copy-start.24
  129.3 1.0 copy-start.2
  139.3 10.0 %copy-start.12 = (bf16[1,8,64,256]{3,2,1,0:T(8,128)(2,1)S(1)}, bf16[1,8,64,256]{3,2,1,0:T(8,128)(2,1)}, u32[]{:S(2)}) copy-start(bf16[1,8,64,256]{3,2,1,0:T(8,128)(2,1)} %param.10) | copy-start | bytes 786436
  141.6 16.3 %copy-start.21 = (bf16[2,128,64]{1,2,0:T(8,128)(2,1)S(1)}, bf16[2,128,64]{1,2,0:T(8,128)(2,1)}, u32[]{:S(2)}) copy-start(bf16[2,128,64]{1,2,0:T(8,128)(2,1)} %param.12) | copy-start | bytes 98308
  141.6 24.3 %copy-start.26 = (f32[128]{0:T(128)S(1)}, f32[128]{0:T(128)}, u32[]{:S(2)}) copy-start(f32[128]{0:T(128)} %param.13) | copy-start | bytes 1540
  141.6 30.6 %all-to-all-start.3 = ((bf16[16,2,16384]{2,1,0:T(2,128)(2,1)}), bf16[16,2,16384]{2,1,0:T(2,128)(2,1)}, u32[]{:S(2)}, u32[]{:S(2)}) async-start(bf16[16,2,16384]{2,1,0:T(2,128)(2,1)} %reshape.260), calls=%async_computation.3 | async-start | bytes 2097152 | tf_op jit(solution)/shard_map/all_to_all | solution.py:127
  149.3 16.6 %collective-permute-start = (bf16[2,64,256]{2,1,0:T(8,128)(2,1)S(1)}, bf16[2,64,256]{2,1,0:T(8,128)(2,1)S(1)}, u32[]{:S(2)}, u32[]{:S(2)}) collective-permute-start(bf16[2,64,256]{2,1,0:T(8,128)(2,1)S(1)} %slice_bitcast_fusion.1), channel_id=1, source_target_pairs={{0,1},{1,2},{2,3},{4,5},{5,6},{6,7},{8,9},{9,10},{10,11},{12,13},{... | collective-permute-start | bytes 196616 | tf_op jit(solution)/shard_map/ppermute | solution.py:13
  157.8 8.1 %copy-start.17 = (bf16[6,64,256]{2,1,0:T(8,128)(2,1)}, bf16[6,64,256]{2,1,0:T(8,128)(2,1)S(1)}, u32[]{:S(2)}) copy-start(bf16[6,64,256]{2,1,0:T(8,128)(2,1)S(1)} %slice_bitcast_fusion) | copy-start | bytes 589828
  250.3 1.2 copy-start.11
  251.9 23.9 %copy-start.5 = (bf16[8,64,256]{2,1,0:T(8,128)(2,1)}, bf16[8,64,256]{2,1,0:T(8,128)(2,1)S(1)}, u32[]{:S(2)}) copy-start(bf16[8,64,256]{2,1,0:T(8,128)(2,1)S(1)} %get-tuple-element.27) | copy-start | bytes 786436
  251.9 23.9 %copy-start.7 = (bf16[8,64,256]{2,1,0:T(8,128)(2,1)}, bf16[8,64,256]{2,1,0:T(8,128)(2,1)S(1)}, u32[]{:S(2)}) copy-start(bf16[8,64,256]{2,1,0:T(8,128)(2,1)S(1)} %get-tuple-element.28) | copy-start | bytes 786436
  265.1 10.2 %copy-start.22 = (s32[2,8]{1,0:T(2,128)S(1)}, s32[2,8]{1,0:T(2,128)}, u32[]{:S(2)}) copy-start(s32[2,8]{1,0:T(2,128)} %param.17) | copy-start | bytes 196
  267.3 8.2 %copy-start.18 = (bf16[6,64,256]{2,1,0:T(8,128)(2,1)S(1)}, bf16[6,64,256]{2,1,0:T(8,128)(2,1)}, u32[]{:S(2)}) copy-start(bf16[6,64,256]{2,1,0:T(8,128)(2,1)} %copy-done.17) | copy-start | bytes 589828
  267.3 8.5 %copy-start.13 = (bf16[1,8,64,256]{3,2,1,0:T(8,128)(2,1)S(1)}, bf16[1,8,64,256]{3,2,1,0:T(8,128)(2,1)}, u32[]{:S(2)}) copy-start(bf16[1,8,64,256]{3,2,1,0:T(8,128)(2,1)} %param.10) | copy-start | bytes 786436
  267.3 30.0 %all-to-all-start = ((bf16[16,2,16384]{2,1,0:T(2,128)(2,1)}), bf16[16,2,16384]{2,1,0:T(2,128)(2,1)S(1)}, u32[]{:S(2)}, u32[]{:S(2)}) async-start(bf16[16,2,16384]{2,1,0:T(2,128)(2,1)} %reshape.254), calls=%async_computation | async-start | bytes 2097152 | tf_op jit(solution)/shard_map/all_to_all | solution.py:106
  306.5 2.3 copy-start.3
  318.0 13.4 %copy-start.6 = (bf16[8,64,256]{2,1,0:T(8,128)(2,1)S(1)}, bf16[8,64,256]{2,1,0:T(8,128)(2,1)}, u32[]{:S(2)}) copy-start(bf16[8,64,256]{2,1,0:T(8,128)(2,1)} %copy-done.5) | copy-start | bytes 786436
  318.0 13.4 %copy-start.8 = (bf16[8,64,256]{2,1,0:T(8,128)(2,1)S(1)}, bf16[8,64,256]{2,1,0:T(8,128)(2,1)}, u32[]{:S(2)}) copy-start(bf16[8,64,256]{2,1,0:T(8,128)(2,1)} %copy-done.7) | copy-start | bytes 786436
  322.7 8.7 %copy-start.10 = (bf16[8,64,256]{2,1,0:T(8,128)(2,1)S(1)}, bf16[8,64,256]{2,1,0:T(8,128)(2,1)}, u32[]{:S(2)}) copy-start(bf16[8,64,256]{2,1,0:T(8,128)(2,1)} %copy-done.9) | copy-start | bytes 786436
  322.7 11.3 %copy-start.14 = (bf16[1,8,64,256]{3,2,1,0:T(8,128)(2,1)S(1)}, bf16[1,8,64,256]{3,2,1,0:T(8,128)(2,1)}, u32[]{:S(2)}) copy-start(bf16[1,8,64,256]{3,2,1,0:T(8,128)(2,1)} %param.10) | copy-start | bytes 786436
  322.7 11.3 %copy-start.25 = (f32[64]{0:T(128)S(1)}, f32[64]{0:T(128)}, u32[]{:S(2)}) copy-start(f32[64]{0:T(128)} %param.15) | copy-start | bytes 772
  322.7 260.2 %all-to-all-start.1 = ((bf16[16,2,16384]{2,1,0:T(2,128)(2,1)}), bf16[16,2,16384]{2,1,0:T(2,128)(2,1)S(1)}, u32[]{:S(2)}, u32[]{:S(2)}) async-start(bf16[16,2,16384]{2,1,0:T(2,128)(2,1)} %reshape.256), calls=%async_computation.1 | async-start | bytes 2097152 | tf_op jit(solution)/shard_map/all_to_all | solution.py:109
  330.6 246.8 %all-reduce.3.cloned.1.call-start = ((), (), s32[]{:S(2)}) async-start(), calls=%async_computation.4 | async-start | bytes 131072 | tf_op jit(solution)/shard_map/psum | solution.py:177
  335.7 245.5 %copy-start.16 = (f32[8,64,256]{2,1,0:T(8,128)S(1)}, f32[8,64,256]{2,1,0:T(8,128)}, u32[]{:S(2)}) copy-start(f32[8,64,256]{2,1,0:T(8,128)} %fusion.4) | copy-start | bytes 1572868
  336.4 242.5 %collective-permute-start.1 = (bf16[2,128,256]{2,1,0:T(8,128)(2,1)}, bf16[2,128,256]{2,1,0:T(8,128)(2,1)}, u32[]{:S(2)}, u32[]{:S(2)}) collective-permute-start(bf16[2,128,256]{2,1,0:T(8,128)(2,1)} %fusion.50), channel_id=1, source_target_pairs={{1,0},{2,1},{3,2},{5,4},{6,5},{7,6},{9,8},{10,9},{11,10},{13,12},{... | collective-permute-start | bytes 393224 | tf_op jit(solution)/shard_map/ppermute | solution.py:13
  592.1 2.3 copy-start.4
  594.4 1.0 copy-start.15
  594.4 2.7 copy-start.20
  (2 other events, 1.4 us)
Sparse Core Ops, SparseCore 0:
  337.6 239.8 all-reduce.2
where the time goes:
time: 688 us; the launch traced here: 681 us
  waiting for transfers between devices  286 us (42%)
  other arithmetic  183 us (27%)
  blocking collectives  75 us (11%)
  local copies, waits for them, and re-layouts  58.8 us (9%)
  starting transfers between devices  45.2 us (7%)
  matrix products  18.1 us (3%)
  between operations  14.7 us (2%)
    psum x1, waiting for transfers between devices, body(): lax.psum((grad_conv_w, grad_conv_b, grad_mix_w, grad_mix_b), ('dp', 'spac...  237 us
    scatter-add x2, other arithmetic, back_finish(): total.at[:, :, send_rows[0]].add(returned * live_slots.astype(jnp.float32))  143 us
    psum x1, blocking collectives, body(): lax.psum((grad_conv_w, grad_conv_b, grad_mix_w, grad_mix_b), ('dp', 'spac...  75 us
    unnamed x63, local copies, waits for them, and re-layouts  26.4 us
    all_to_all x1, waiting for transfers between devices, body(): lax.all_to_all(packed_one, 'space', split_axis=2, concat_axis=2, tiled=True)  21.2 us
    all_to_all x1, waiting for transfers between devices, body(): lax.all_to_all(back_start(back_two, adj_tiles, tile_cols, send_rows), 'sp...  18.7 us
  transfers between devices with their start and end apart: 7, of which 5 were waited for; matrix products, arithmetic and copies ran while one was open for 3% of the time, Pallas kernels for 0%

commit v1 on v0

--- a/solution.py
+++ b/solution.py
@@ -175,7 +175,7 @@
     )
     grad_conv_b = jnp.sum(backward_preactivation.astype(jnp.float32), axis=(0, 2))
     grad_conv_w, grad_conv_b, grad_mix_w, grad_mix_b = lax.psum(
-        (grad_conv_w, grad_conv_b, grad_mix_w, grad_mix_b), ("dp", "space", "tm")
+        lax.psum((grad_conv_w, grad_conv_b, grad_mix_w, grad_mix_b), "dp"), ("space", "tm")
     )
     cell_count = (
         inputs.shape[0]

time: 688 us -> 909 us (1.32)
  the two profiles are of different devices: /device:TPU:1 before, /device:TPU:32 now
where the time goes in v1:
time: 909 us; the launch traced here: 901 us
  blocking collectives  322 us (35%)
  waiting for transfers between devices  278 us (31%)
  other arithmetic  183 us (20%)
  local copies, waits for them, and re-layouts  58.6 us (6%)
  starting transfers between devices  27.6 us (3%)
  matrix products  17.3 us (2%)
  between operations  14.7 us (2%)
    psum x1, blocking collectives, body(): lax.psum(lax.psum((grad_conv_w, grad_conv_b, grad_mix_w, grad_mix_b), 'dp...  304 us
    psum x1, waiting for transfers between devices, body(): lax.psum(lax.psum((grad_conv_w, grad_conv_b, grad_mix_w, grad_mix_b), 'dp...  168 us
    scatter-add x2, other arithmetic, back_finish(): total.at[:, :, send_rows[0]].add(returned * live_slots.astype(jnp.float32))  143 us
    psum x1, waiting for transfers between devices, body(): lax.psum((grad_conv_w, grad_conv_b, grad_mix_w, grad_mix_b), 'dp')  46.1 us
    unnamed x69, local copies, waits for them, and re-layouts  26.4 us
    all_to_all x1, waiting for transfers between devices, body(): lax.all_to_all(packed_one, 'space', split_axis=2, concat_axis=2, tiled=True)  23.3 us
    all_to_all x1, waiting for transfers between devices, body(): lax.all_to_all(back_start(back_two, adj_tiles, tile_cols, send_rows), 'sp...  22.2 us
    all_to_all x1, waiting for transfers between devices, body(): lax.all_to_all(back_start(back_one, adj_tiles, tile_cols, send_rows), 'sp...  18.7 us
  transfers between devices with their start and end apart: 8, of which 5 were waited for; matrix products, arithmetic and copies ran while one was open for 2% of the time, Pallas kernels for 0%

profile of v1, /device:TPU:32, one launch (start us, length us, event | category | flops | bytes accessed | tf_op | source)
XLA Modules:
  0.0 901.4 jit_solution(8544538356201334967)
XLA Ops:
  12.5 3.5 scatter_fusion.1
  19.6 8.7 all-to-all-start.2
  31.9 22.2 %all-to-all-done.2 = bf16[16,2,16384]{2,1,0:T(2,128)(2,1)} async-done(((bf16[16,2,16384]{2,1,0:T(2,128)(2,1)}), bf16[16,2,16384]{2,1,0:T(2,128)(2,1)}, u32[]{:S(2)}, u32[]{:S(2)}) %all-to-all-start.2) | async-done | bytes 1048608 | tf_op jit(solution)/shard_map/all_to_all | solution.py:116
  54.1 3.8 reshape.259
  57.8 3.1 convert_multiply_fusion.1
  61.0 71.3 %scatter_fusion.2 = f32[8,64,256]{1,0,2:T(8,128)S(1)} fusion(f32[8,64,256]{1,0,2:T(8,128)S(1)} %copy.84, s32[1024]{0:T(1024)S(1)} %reshape.131, f32[1024,8,64]{2,1,0:T(8,128)} %bitcast.273), kind=kCustom, calls=%fused_computation.6 | custom fusion | flops 524288 | bytes 6295552 | tf_op jit(solution)/shard_map/scatter-add | solution.py:73
  135.4 3.5 scatter_fusion.4
  144.5 5.3 all-to-all-start.3
  156.6 18.7 %all-to-all-done.3 = bf16[16,2,16384]{2,1,0:T(2,128)(2,1)} async-done(((bf16[16,2,16384]{2,1,0:T(2,128)(2,1)}), bf16[16,2,16384]{2,1,0:T(2,128)(2,1)}, u32[]{:S(2)}, u32[]{:S(2)}) %all-to-all-start.3) | async-done | bytes 1048608 | tf_op jit(solution)/shard_map/all_to_all | solution.py:127
  175.3 3.8 reshape.261
  179.1 3.1 convert_multiply_fusion
  182.2 71.3 %scatter_fusion.5 = f32[8,64,256]{1,0,2:T(8,128)S(1)} fusion(f32[8,64,256]{1,0,2:T(8,128)S(1)} %copy.92, s32[1024]{0:T(1024)S(1)} %reshape.131, f32[1024,8,64]{2,1,0:T(8,128)} %bitcast.272), kind=kCustom, calls=%fused_computation.9 | custom fusion | flops 524288 | bytes 6295552 | tf_op jit(solution)/shard_map/scatter-add | solution.py:73
  255.7 7.6 gather_fusion
  263.3 4.9 fusion.76
  270.5 5.2 all-to-all-start
  277.2 23.3 %all-to-all-done = bf16[16,2,16384]{2,1,0:T(2,128)(2,1)S(1)} async-done(((bf16[16,2,16384]{2,1,0:T(2,128)(2,1)}), bf16[16,2,16384]{2,1,0:T(2,128)(2,1)S(1)}, u32[]{:S(2)}, u32[]{:S(2)}) %all-to-all-start) | async-done | bytes 1048608 | tf_op jit(solution)/shard_map/all_to_all | solution.py:106
  300.5 2.3 reshape.255
  302.8 3.4 pad_maximum_fusion
  306.2 3.3 copy.65
  309.5 2.3 gather_fusion.1
  312.9 3.3 gather_fusion.2
  316.2 4.8 fusion.77
  321.0 4.7 reshape.256
  325.7 5.3 all-to-all-start.1
  334.6 46.1 %all-reduce.5.cloned.1.call-done = f32[2,128,64]{1,2,0:T(8,128)} async-done(((f32[2,128,64]{1,2,0:T(8,128)}), f32[2,128,64]{1,2,0:T(8,128)}) %all-reduce.5.cloned.1.call-update) | async-done | bytes 65552 | tf_op jit(solution)/shard_map/psum | solution.py:178
  383.2 168.0 %all-reduce.7.cloned.1.call-done = f32[2,128,64]{1,2,0:T(8,128)} async-done(((f32[2,128,64]{1,2,0:T(8,128)}), f32[2,128,64]{1,2,0:T(8,128)}) %all-reduce.7.cloned.1.call-update) | async-done | bytes 65552 | tf_op jit(solution)/shard_map/psum | solution.py:177
  556.7 2.3 reshape.257
  559.0 3.4 pad_maximum_fusion.1
  562.4 3.3 copy.71
  565.7 2.3 gather_fusion.3
  570.8 18.1 %all-reduce.1 = (f32[128]{0:T(128)S(1)}, f32[3,64,64]{1,2,0:T(8,128)S(1)}, f32[64]{0:T(128)S(1)}) all-reduce(f32[128]{0:T(128)S(1)} %convert_reduce_fusion, f32[3,64,64]{1,2,0:T(8,128)S(1)} %pad_maximum_fusion.6, f32[64]{0:T(128)S(1)} %convert_reduce_fusion.1), channel_id=1, replica_groups=mesh['dp'=4,'space'=16,'tm'=4] {'dp'}, use_global_device_ids=true, to_apply=%region_9.0 | all-reduce | flops 12480 | bytes 99840 | tf_op jit(solution)/shard_map/psum | solution.py:178
  588.9 303.9 %all-reduce = (f32[128]{0:T(128)S(1)}, f32[3,64,64]{1,2,0:T(8,128)S(1)}, f32[64]{0:T(128)S(1)}) all-reduce(f32[128]{0:T(128)S(1)} %get-tuple-element.27, f32[3,64,64]{1,2,0:T(8,128)S(1)} %get-tuple-element.28, f32[64]{0:T(128)S(1)} %get-tuple-element.29), channel_id=1, replica_groups=mesh['dp'=4,'space'=16,'tm'=4] {'space','tm'}, use_global_device_ids=true, to_apply=%region_10.0 | all-reduce | flops 12480 | bytes 99840 | tf_op jit(solution)/shard_map/psum | solution.py:177
  (145 shorter events, 50.8 us)
Async XLA Ops:
  17.3 11.0 %copy-start.1 = (bf16[2,8,128,128]{3,2,1,0:T(8,128)(2,1)S(1)}, bf16[2,8,128,128]{3,2,1,0:T(8,128)(2,1)}, u32[]{:S(2)}) copy-start(bf16[2,8,128,128]{3,2,1,0:T(8,128)(2,1)} %param.16) | copy-start | bytes 1572868
  19.6 34.5 %all-to-all-start.2 = ((bf16[16,2,16384]{2,1,0:T(2,128)(2,1)}), bf16[16,2,16384]{2,1,0:T(2,128)(2,1)}, u32[]{:S(2)}, u32[]{:S(2)}) async-start(bf16[16,2,16384]{2,1,0:T(2,128)(2,1)} %reshape.258), calls=%async_computation.2 | async-start | bytes 2097152 | tf_op jit(solution)/shard_map/all_to_all | solution.py:116
  29.0 1.9 copy-start
  29.1 1.9 copy-start.19
  142.2 7.5 copy-start.12
  144.5 7.1 copy-start.21
  144.5 7.5 copy-start.29
  144.5 30.8 %all-to-all-start.3 = ((bf16[16,2,16384]{2,1,0:T(2,128)(2,1)}), bf16[16,2,16384]{2,1,0:T(2,128)(2,1)}, u32[]{:S(2)}, u32[]{:S(2)}) async-start(bf16[16,2,16384]{2,1,0:T(2,128)(2,1)} %reshape.260), calls=%async_computation.3 | async-start | bytes 2097152 | tf_op jit(solution)/shard_map/all_to_all | solution.py:127
  149.8 2.2 collective-permute-start
  151.6 1.7 copy-start.17
  152.0 1.3 copy-start.22
  255.0 21.2 %copy-start.5 = (bf16[8,64,256]{2,1,0:T(8,128)(2,1)}, bf16[8,64,256]{2,1,0:T(8,128)(2,1)S(1)}, u32[]{:S(2)}) copy-start(bf16[8,64,256]{2,1,0:T(8,128)(2,1)S(1)} %get-tuple-element.30) | copy-start | bytes 786436
  255.0 21.2 %copy-start.7 = (bf16[8,64,256]{2,1,0:T(8,128)(2,1)}, bf16[8,64,256]{2,1,0:T(8,128)(2,1)S(1)}, u32[]{:S(2)}) copy-start(bf16[8,64,256]{2,1,0:T(8,128)(2,1)S(1)} %get-tuple-element.31) | copy-start | bytes 786436
  268.2 7.5 copy-start.25
  270.5 5.5 copy-start.18
  270.5 5.5 copy-start.23
  270.5 5.8 copy-start.13
  270.5 30.0 %all-to-all-start = ((bf16[16,2,16384]{2,1,0:T(2,128)(2,1)}), bf16[16,2,16384]{2,1,0:T(2,128)(2,1)S(1)}, u32[]{:S(2)}, u32[]{:S(2)}) async-start(bf16[16,2,16384]{2,1,0:T(2,128)(2,1)} %reshape.254), calls=%async_computation | async-start | bytes 2097152 | tf_op jit(solution)/shard_map/all_to_all | solution.py:106
  309.5 2.3 copy-start.3
  321.0 10.0 %copy-start.24 = (f32[1,128,64]{1,2,0:T(8,128)S(1)}, f32[1,128,64]{1,2,0:T(8,128)}, u32[]{:S(2)}) copy-start(f32[1,128,64]{1,2,0:T(8,128)} %convolution_bitcast_fusion.13) | copy-start | bytes 98308
  321.0 10.7 %copy-start.10 = (bf16[8,64,256]{2,1,0:T(8,128)(2,1)S(1)}, bf16[8,64,256]{2,1,0:T(8,128)(2,1)}, u32[]{:S(2)}) copy-start(bf16[8,64,256]{2,1,0:T(8,128)(2,1)} %copy-done.9) | copy-start | bytes 786436
  325.7 6.9 copy-start.6
  325.7 6.9 copy-start.8
  325.7 7.9 copy-start.14
  325.7 7.9 copy-start.28
  325.7 231.0 %all-to-all-start.1 = ((bf16[16,2,16384]{2,1,0:T(2,128)(2,1)}), bf16[16,2,16384]{2,1,0:T(2,128)(2,1)S(1)}, u32[]{:S(2)}, u32[]{:S(2)}) async-start(bf16[16,2,16384]{2,1,0:T(2,128)(2,1)} %reshape.256), calls=%async_computation.1 | async-start | bytes 2097152 | tf_op jit(solution)/shard_map/all_to_all | solution.py:109
  331.0 49.8 %all-reduce.5.cloned.1.call-start = ((), (), s32[]{:S(2)}) async-start(), calls=%async_computation.4 | async-start | bytes 131072 | tf_op jit(solution)/shard_map/psum | solution.py:178
  331.7 219.5 %all-reduce.7.cloned.1.call-start = ((), (), s32[]{:S(2)}) async-start(), calls=%async_computation.5 | async-start | bytes 131072 | tf_op jit(solution)/shard_map/psum | solution.py:177
  334.6 220.4 %copy-start.16 = (f32[8,64,256]{2,1,0:T(8,128)S(1)}, f32[8,64,256]{2,1,0:T(8,128)}, u32[]{:S(2)}) copy-start(f32[8,64,256]{2,1,0:T(8,128)} %fusion.4) | copy-start | bytes 1572868
  381.4 171.2 %collective-permute-start.1 = (bf16[2,128,256]{2,1,0:T(8,128)(2,1)}, bf16[2,128,256]{2,1,0:T(8,128)(2,1)}, u32[]{:S(2)}, u32[]{:S(2)}) collective-permute-start(bf16[2,128,256]{2,1,0:T(8,128)(2,1)} %fusion.50), channel_id=1, source_target_pairs={{1,0},{2,1},{3,2},{5,4},{6,5},{7,6},{9,8},{10,9},{11,10},{13,12},{... | collective-permute-start | bytes 393224 | tf_op jit(solution)/shard_map/ppermute | solution.py:13
  565.7 2.3 copy-start.4
  568.1 2.7 copy-start.20
  (6 other events, 5.5 us)
Sparse Core Ops, SparseCore 0:
  334.7 46.0 all-reduce.4
  384.6 166.5 all-reduce.6
